TPU v7x, 512 devices: a whole 4x8x8 slice. The times are simulated.
512 devices in a mesh: dp: 256 (over z, y, x), ctx: 2 (over core).
Axes of the slice: x: 4, y: 8, z: 8, core: 2. Of those that a mesh axis runs over, the one named last changes fastest.
Arguments:
- head_inputs: bfloat16 [256, 512, 1024], P('dp', 'ctx'), may hold values from -6 to 6
- cotangent: bfloat16 [256, 512, 1024], P('dp', 'ctx'), may hold values from -6 to 6
- write_proj: bfloat16 [256, 512, 256], P('dp', 'ctx'), may hold values from -3 to 3
- read_proj: bfloat16 [256, 512, 256], P('dp', 'ctx'), may hold values from -3 to 3
- step_raw: float32 [256, 512, 16], P('dp', 'ctx'), may hold values from -4 to 4
- doc_index: int32 [256, 512], P('dp', 'ctx'), may hold values from 0 to 15, never falling along the last dimension, each value on 1 to 257 neighbouring positions
- log_rate: float32 [16], replicated, may hold values from 0 to 2.77
- step_bias: float32 [16], replicated, may hold values from -6.9 to -2.25
- skip_gain: float32 [16], replicated, may hold values from 0.5 to 1.5
Outputs:
- grad_inputs: bfloat16 [256, 512, 1024], P('dp', 'ctx')
- grad_write: bfloat16 [256, 512, 256], P('dp', 'ctx')
- grad_read: bfloat16 [256, 512, 256], P('dp', 'ctx')
- grad_step: float32 [256, 512, 16], P('dp', 'ctx')
- grad_rate: float32 [16], replicated
- grad_bias: float32 [16], replicated
- grad_skip: float32 [16], replicated
Inputs may be any that keep to these rules, and one draw needn't show every extreme that they name: doc_index never falls along a sequence; each document spans 1 to 257 tokens and one of each sequence spans exactly that many.
All inputs are finite; a program needn't handle non-finite values.
Results may differ from a plain program's by a relative error of at most 0.0025.
Values may be sent and summed in bfloat16 or wider, within the bound.
No kernel may reach another device: no remote copies, remote signals or barrier semaphores. Data moves between devices by JAX's collectives and lax.ppermute only.
A program may use at most 64 MiB of HBM per device.

v0:
```python
import jax
import jax.numpy as jnp
from jax import lax
from jax.sharding import PartitionSpec as P

HEADS = 16
HEAD_DIM = 64
STATE = 256
BLOCK = 256


def ssd_forward(
    inputs, writes, reads, steps, segment, segment_prev, state_init, log_rate, skip_gain
):
    length, heads, width = inputs.shape
    count = length // BLOCK
    rate_all = steps * (-jnp.exp(log_rate))[None, :]
    blocks = (
        inputs.reshape(count, BLOCK, heads, width),
        writes.reshape(count, BLOCK, -1),
        reads.reshape(count, BLOCK, -1),
        steps.reshape(count, BLOCK, heads),
        rate_all.reshape(count, BLOCK, heads),
        segment.reshape(count, BLOCK),
    )
    causal = jnp.arange(BLOCK)[:, None] >= jnp.arange(BLOCK)[None, :]
    highest = lax.Precision.HIGHEST

    def advance(carry, piece):
        state, last_doc = carry
        in_block, write_block, read_block, step_block, rate_block, doc_block = piece
        cumulative = jnp.cumsum(rate_block, axis=0)
        same_doc = causal & (doc_block[:, None] == doc_block[None, :])
        gaps = cumulative[:, None, :] - cumulative[None, :, :]
        decay = jnp.exp(jnp.where(same_doc[:, :, None], gaps, -1e30))
        scores = jnp.einsum("in,jn->ij", read_block, write_block, precision=highest)
        mixing = decay * (scores[:, :, None] * step_block[None, :, :])
        result = jnp.einsum("ijh,jhp->ihp", mixing, in_block, precision=highest)
        keep = (doc_block == last_doc).astype(jnp.float32)
        start = jnp.exp(cumulative) * keep[:, None]
        result = (
            result
            + jnp.einsum("in,hpn->ihp", read_block, state, precision=highest) * start[:, :, None]
        )
        result = result + skip_gain[None, :, None] * in_block
        end_doc = doc_block[BLOCK - 1]
        tail = (
            jnp.exp(cumulative[BLOCK - 1][None, :] - cumulative)
            * (doc_block == end_doc).astype(jnp.float32)[:, None]
            * step_block
        )
        carried = jnp.exp(cumulative[BLOCK - 1]) * (end_doc == last_doc).astype(jnp.float32)
        state = carried[:, None, None] * state + jnp.einsum(
            "jh,jhp,jn->hpn", tail, in_block, write_block, precision=highest
        )
        return ((state, end_doc), result)

    (state, _), results = lax.scan(jax.checkpoint(advance), (state_init, segment_prev), blocks)
    return (results.reshape(length, heads, width), state)


def layer_grads(
    inputs,
    cotangent,
    writes,
    reads,
    step_raw,
    segment,
    segment_prev,
    state_init,
    log_rate,
    step_bias,
    skip_gain,
    state_grad,
):
    length = inputs.shape[0]
    heads = step_raw.shape[1]
    head_view = inputs.astype(jnp.float32).reshape(length, heads, HEAD_DIM)

    def forward(head_view, writes, reads, step_raw, log_rate, step_bias, skip_gain):
        steps = jax.nn.softplus(step_raw + step_bias[None, :])
        return ssd_forward(
            head_view, writes, reads, steps, segment, segment_prev, state_init, log_rate, skip_gain
        )

    _, pullback = jax.vjp(
        forward,
        head_view,
        writes.astype(jnp.float32),
        reads.astype(jnp.float32),
        step_raw,
        log_rate,
        step_bias,
        skip_gain,
    )
    return pullback((cotangent.astype(jnp.float32).reshape(length, heads, HEAD_DIM), state_grad))


def on_device(
    head_inputs,
    cotangent,
    write_proj,
    read_proj,
    step_raw,
    doc_index,
    log_rate,
    step_bias,
    skip_gain,
):
    group_size = lax.axis_size("ctx")
    per_device = HEADS // group_size
    first_head = lax.axis_index("ctx") * per_device
    head_rows, cotan_rows = (
        lax.all_to_all(head_inputs, "ctx", split_axis=2, concat_axis=1, tiled=True),
        lax.all_to_all(cotangent, "ctx", split_axis=2, concat_axis=1, tiled=True),
    )
    raw_steps = lax.all_to_all(step_raw, "ctx", split_axis=2, concat_axis=1, tiled=True)
    write_all, read_all = (
        lax.all_gather(write_proj, "ctx", axis=1, tiled=True),
        lax.all_gather(read_proj, "ctx", axis=1, tiled=True),
    )
    segment = lax.all_gather(doc_index, "ctx", axis=1, tiled=True)[0]
    length = segment.shape[0]
    rate_here = lax.dynamic_slice_in_dim(log_rate, first_head, per_device)
    bias_here = lax.dynamic_slice_in_dim(step_bias, first_head, per_device)
    skip_here = lax.dynamic_slice_in_dim(skip_gain, first_head, per_device)
    zero_state = jnp.zeros((per_device, HEAD_DIM, STATE), jnp.float32)
    grads = layer_grads(
        head_rows[0],
        cotan_rows[0],
        write_all[0],
        read_all[0],
        raw_steps[0],
        segment,
        segment[0],
        zero_state,
        rate_here,
        bias_here,
        skip_here,
        zero_state,
    )
    out_inputs = lax.all_to_all(
        grads[0].reshape(1, length, per_device * HEAD_DIM).astype(jnp.bfloat16),
        "ctx",
        split_axis=1,
        concat_axis=2,
        tiled=True,
    )
    out_step = lax.all_to_all(grads[3][None], "ctx", split_axis=1, concat_axis=2, tiled=True)
    sum_write, sum_read = (
        lax.psum_scatter(grads[1][None], "ctx", scatter_dimension=1, tiled=True),
        lax.psum_scatter(grads[2][None], "ctx", scatter_dimension=1, tiled=True),
    )
    out_write = sum_write.astype(jnp.bfloat16)
    out_read = sum_read.astype(jnp.bfloat16)

    def place(values):
        return lax.dynamic_update_slice_in_dim(
            jnp.zeros((HEADS,), jnp.float32), values, first_head, 0
        )

    partial_sums = (place(grads[4]), place(grads[5]), place(grads[6]))
    total_rate, total_bias, total_skip = lax.psum(
        (partial_sums[0], partial_sums[1], partial_sums[2]), ("dp", "ctx")
    )
    return (out_inputs, out_write, out_read, out_step, total_rate, total_bias, total_skip)


def solution(mesh):
    placed = (
        P("dp", "ctx", None),
        P("dp", "ctx", None),
        P("dp", "ctx", None),
        P("dp", "ctx", None),
        P("dp", "ctx", None),
        P("dp", "ctx"),
        P(),
        P(),
        P(),
    )
    return jax.shard_map(
        on_device,
        mesh=mesh,
        in_specs=placed,
        out_specs=(
            P("dp", "ctx", None),
            P("dp", "ctx", None),
            P("dp", "ctx", None),
            P("dp", "ctx", None),
            P(),
            P(),
            P(),
        ),
        check_vma=False,
    )
```

profile of v0, /device:TPU:1, one launch (start us, length us, event | category | flops | bytes accessed | tf_op | source)
XLA Modules:
  0.0 267.5 jit_solution(3828304413454677464)
XLA Ops:
  7.2 2.4 copy.57
  10.2 3.9 %reduce.18 = bf16[1024,256]{1,0:T(8,128)(2,1)S(1)} reduce(bf16[1024,1,256]{2,1,0:T(2,128)(2,1)S(1)} %bitcast.276, bf16[]{:T(256)} %broadcast.266), dimensions={1}, to_apply=%bitcast.160.reduce_sub_computation | reduce | bytes 1048578
  15.0 10.5 %all-to-all-start.1 = ((bf16[2,2,65536]{2,1,0:T(2,128)(2,1)}), bf16[2,2,65536]{2,1,0:T(2,128)(2,1)S(1)}, u32[]{:S(2)}, u32[]{:S(2)}) async-start(bf16[2,2,65536]{2,1,0:T(2,128)(2,1)} %reshape.420), calls=%async_computation.1 | async-start | bytes 1048576 | tf_op jit(solution)/shard_map/all_to_all | solution.py:114
  26.2 1.8 all_gather.9
  30.4 2.0 all_gather.10
  32.4 2.0 all_gather.11
  34.4 2.4 copy.58
  36.8 4.7 %reduce.19 = bf16[1024,256]{1,0:T(8,128)(2,1)} reduce(bf16[1024,1,256]{2,1,0:T(2,128)(2,1)S(1)} %bitcast.280, bf16[]{:T(256)} %broadcast.266), dimensions={1}, to_apply=%bitcast.162.reduce_sub_computation | reduce | bytes 1048578
  41.5 1.8 reshape.422
  43.3 4.4 %all-to-all-start.2 = ((bf16[2,2,65536]{2,1,0:T(2,128)(2,1)}), bf16[2,2,65536]{2,1,0:T(2,128)(2,1)}, u32[]{:S(2)}, u32[]{:S(2)}) async-start(bf16[2,2,65536]{2,1,0:T(2,128)(2,1)} %reshape.422), calls=%async_computation.2 | async-start | bytes 1048576 | tf_op jit(solution)/shard_map/all_to_all | solution.py:115
  48.2 1.1 convert_bitcast_fusion.1
  49.3 1.1 copy.72
  50.4 3.3 %all-to-all-start = ((f32[1,256,16]{1,0,2:T(1,128)}), f32[1,256,16]{1,0,2:T(1,128)S(1)}, u32[]{:S(2)}, u32[]{:S(2)}) async-start(f32[1,256,16]{1,0,2:T(1,128)} %copy.56), calls=%async_computation | async-start | bytes 32768 | tf_op jit(solution)/shard_map/all_to_all | solution.py:117
  53.8 1.4 reshape.423
  55.3 1.1 convert_bitcast_fusion
  56.4 1.1 copy.73
  58.1 13.2 %while.44 = (s32[]{:T(128)}, f32[8,64,256]{2,1,0:T(8,128)S(1)}, s32[]{:T(128)}, f32[2,8,64,256]{3,2,1,0:T(8,128)}, s32[2]{0:T(128)S(1)}, /*index=5*/f32[2,256,8]...) while((s32[]{:T(128)}, f32[8,64,256]{2,1,0:T(8,128)S(1)}, ...), condition=%wide.region_3.4_spmd.clone, body=%wide.region_0.3_spmd.clone.sunk | while | flops 403577376 | bytes 2971505 | solution.py:58
  62.8 1.9 convolution_add_fusion.6
  69.4 1.9 convolution_add_fusion.6
  75.0 60.5 %while.45 = (s32[]{:T(128)}, f32[8]{0:T(128)}, f32[8,64,256]{2,1,0:T(8,128)}, bf16[2,256,8,64]{1,3,2,0:T(8,128)(2,1)}, f32[2,256,256]{2,1,0:T(8,128)}, /*index=5...) while((s32[]{:T(128)}, f32[8]{0:T(128)}, ...), condition=%wide.region_17.18_spmd.clone, body=%wide.region_4.0_spmd.clone.sunk | while | flops 3434652672 | bytes 35708892 | solution.py:58
  75.8 1.2 dynamic-slice_bitcast_fusion.14
  77.2 1.1 dynamic-slice_bitcast_fusion.15
  81.1 1.3 compare_convert_fusion.6
  86.1 4.1 %fusion.109 = (f32[256,8]{0,1:T(8,128)}, f32[256,8]{0,1:T(8,128)}, f32[256,8]{0,1:T(8,128)}, f32[256,256]{1,0:T(8,128)S(1)}) fusion(f32[256,8]{0,1:T(8,128)S(1)} %get-tuple-element.914, f32[256,256]{1,0:T(8,128)S(1)} %fusion.108, f32[256,8]{0,1:T(8,128)S(1)} %get-tuple-element.912, pred[256,256]{1,0:T(8,128)(4,1)S(1)} %compare_and_fusion.2, ...), kind=kOutput, calls=%fused_computation.30.clone.1 | convolution fusion | flops 409397248 | bytes 1679360 | tf_op jit(solution)/shard_map/transpose(jvp())/while/body/eval_jaxpr/checkpoint/ijh,jhp->ihp/dot_general | solution.py:38
  90.2 1.1 fusion.114
  93.4 1.4 bitcast_dynamic-update-slice_fusion.7
  94.8 3.6 %fusion.112 = bf16[2,256,8,64]{1,3,2,0:T(8,128)(2,1)} fusion(bf16[2,256,8,64]{1,3,2,0:T(8,128)(2,1)} %get-tuple-element.993, s32[]{:T(128)S(6)} %sub.194, f32[256,8]{0,1:T(8,128)S(1)} %get-tuple-element.914, f32[256,256]{1,0:T(8,128)} %copy-done.1, f32[256,8]{0,1:T(8,128)S(1)} %get-tuple-element.912, pred[256,256]{1,0:T(8,128)(4,1)S(1)} %compare_and_fusion.2, ...), kind=kOutput, calls=%fused_computation.33.clone.1 | convolution fusion | flops 405274624 | bytes 2458116 | tf_op jit(solution)/shard_map/transpose(jvp())/while/body/eval_jaxpr/checkpoint/ijh,jhp->ihp/dot_general | solution.py:38
  98.3 1.0 convolution_bitcast_fusion.4
  99.4 1.4 convolution_add_fusion.7
  101.4 2.5 reduce-window.70
  105.5 1.1 broadcast_select_fusion.3
  106.6 1.2 dynamic-slice_bitcast_fusion.14
  108.0 1.1 dynamic-slice_bitcast_fusion.15
  111.9 1.3 compare_convert_fusion.6
  116.9 4.0 %fusion.109 = (f32[256,8]{0,1:T(8,128)}, f32[256,8]{0,1:T(8,128)}, f32[256,8]{0,1:T(8,128)}, f32[256,256]{1,0:T(8,128)S(1)}) fusion(f32[256,8]{0,1:T(8,128)S(1)} %get-tuple-element.914, f32[256,256]{1,0:T(8,128)S(1)} %fusion.108, f32[256,8]{0,1:T(8,128)S(1)} %get-tuple-element.912, pred[256,256]{1,0:T(8,128)(4,1)S(1)} %compare_and_fusion.2, ...), kind=kOutput, calls=%fused_computation.30.clone.1 | convolution fusion | flops 409397248 | bytes 1679360 | tf_op jit(solution)/shard_map/transpose(jvp())/while/body/eval_jaxpr/checkpoint/ijh,jhp->ihp/dot_general | solution.py:38
  120.9 1.1 fusion.114
  124.1 1.4 bitcast_dynamic-update-slice_fusion.7
  125.5 3.6 %fusion.112 = bf16[2,256,8,64]{1,3,2,0:T(8,128)(2,1)} fusion(bf16[2,256,8,64]{1,3,2,0:T(8,128)(2,1)} %get-tuple-element.993, s32[]{:T(128)S(6)} %sub.194, f32[256,8]{0,1:T(8,128)S(1)} %get-tuple-element.914, f32[256,256]{1,0:T(8,128)} %copy-done.1, f32[256,8]{0,1:T(8,128)S(1)} %get-tuple-element.912, pred[256,256]{1,0:T(8,128)(4,1)S(1)} %compare_and_fusion.2, ...), kind=kOutput, calls=%fused_computation.33.clone.1 | convolution fusion | flops 405274624 | bytes 2458116 | tf_op jit(solution)/shard_map/transpose(jvp())/while/body/eval_jaxpr/checkpoint/ijh,jhp->ihp/dot_general | solution.py:38
  130.2 1.4 convolution_add_fusion.7
  132.2 2.5 reduce-window.70
  137.2 1.3 reduce.21
  140.1 3.3 %all-to-all-start.4 = ((f32[2,1,2048]{2,1,0:T(1,128)}), f32[2,1,2048]{2,1,0:T(1,128)S(1)}, u32[]{:S(2)}, u32[]{:S(2)}) async-start(f32[2,1,2048]{2,1,0:T(1,128)} %reshape.426), calls=%async_computation.6 | async-start | bytes 32768 | tf_op jit(solution)/shard_map/all_to_all | solution.py:149
  143.4 99.9 %all-reduce.2 = (f32[16]{0:T(128)}, f32[16]{0:T(128)}, f32[16]{0:T(128)}) all-reduce(f32[16]{0:T(128)S(1)} %multiply_dynamic-update-slice_fusion, f32[16]{0:T(128)S(1)} %dynamic_update_slice.66, f32[16]{0:T(128)S(1)} %dynamic_update_slice.67), channel_id=1, replica_groups=mesh['dp'=256,'ctx'=2] {'dp','ctx'}, use_global_device_ids=true, to_apply=%region_21.22 | all-reduce | flops 48 | bytes 384 | tf_op jit(solution)/shard_map/psum | solution.py:163
  244.6 3.9 %reduce.20 = bf16[512,512]{1,0:T(8,128)(2,1)S(1)} reduce(bf16[512,1,512]{2,1,0:T(2,128)(2,1)S(1)} %bitcast.277, bf16[]{:T(256)} %broadcast.266), dimensions={1}, to_apply=%bitcast.164.reduce_sub_computation | reduce | bytes 1048578
  248.4 1.1 reshape.424
  249.5 4.2 %all-to-all-start.3 = ((bf16[2,2,65536]{2,1,0:T(2,128)(2,1)}), bf16[2,2,65536]{2,1,0:T(2,128)(2,1)S(1)}, u32[]{:S(2)}, u32[]{:S(2)}) async-start(bf16[2,2,65536]{2,1,0:T(2,128)(2,1)} %reshape.424), calls=%async_computation.3 | async-start | bytes 1048576 | tf_op jit(solution)/shard_map/all_to_all | solution.py:142
  257.4 1.6 convert_element_type.114
  259.0 1.6 convert_element_type.115
  (252 shorter events, 44.6 us)
Async XLA Ops:
  14.0 11.4 %copy-start.32 = (f32[16]{0:T(128)S(1)}, f32[16]{0:T(128)}, u32[]{:S(2)}) copy-start(f32[16]{0:T(128)} %param.20) | copy-start | bytes 196
  14.1 11.5 %copy-start.30 = (f32[16]{0:T(128)S(1)}, f32[16]{0:T(128)}, u32[]{:S(2)}) copy-start(f32[16]{0:T(128)} %param.19) | copy-start | bytes 196
  14.1 11.6 %copy-start.33 = (f32[16]{0:T(128)S(1)}, f32[16]{0:T(128)}, u32[]{:S(2)}) copy-start(f32[16]{0:T(128)} %param.21) | copy-start | bytes 196
  14.1 12.2 %copy-start.29 = (s32[1,256]{1,0:T(1,128)S(1)}, s32[1,256]{1,0:T(1,128)}, u32[]{:S(2)}) copy-start(s32[1,256]{1,0:T(1,128)} %param.18) | copy-start | bytes 3076
  14.1 15.6 %copy-start.20 = (f32[1,256,16]{1,2,0:T(8,128)S(1)}, f32[1,256,16]{1,2,0:T(8,128)}, u32[]{:S(2)}) copy-start(f32[1,256,16]{1,2,0:T(8,128)} %param.17) | copy-start | bytes 49156
  14.1 16.3 %copy-start.16 = (bf16[1,256,256]{2,1,0:T(8,128)(2,1)S(1)}, bf16[1,256,256]{2,1,0:T(8,128)(2,1)}, u32[]{:S(2)}) copy-start(bf16[1,256,256]{2,1,0:T(8,128)(2,1)} %param.15) | copy-start | bytes 393220
  15.0 17.4 %copy-start.17 = (bf16[1,256,256]{2,1,0:T(8,128)(2,1)S(1)}, bf16[1,256,256]{2,1,0:T(8,128)(2,1)}, u32[]{:S(2)}) copy-start(bf16[1,256,256]{2,1,0:T(8,128)(2,1)} %param.16) | copy-start | bytes 393220
  15.0 28.3 %all-to-all-start.1 = ((bf16[2,2,65536]{2,1,0:T(2,128)(2,1)}), bf16[2,2,65536]{2,1,0:T(2,128)(2,1)S(1)}, u32[]{:S(2)}, u32[]{:S(2)}) async-start(bf16[2,2,65536]{2,1,0:T(2,128)(2,1)} %reshape.420), calls=%async_computation.1 | async-start | bytes 1048576 | tf_op jit(solution)/shard_map/all_to_all | solution.py:114
  25.6 31.9 %copy-start.25 = (f32[8]{0:T(128)}, f32[8]{0:T(128)S(1)}, u32[]{:S(2)}) copy-start(f32[8]{0:T(128)S(1)} %dynamic_slice.111) | copy-start | bytes 100
  25.6 31.8 %copy-start.27 = (f32[8]{0:T(128)}, f32[8]{0:T(128)S(1)}, u32[]{:S(2)}) copy-start(f32[8]{0:T(128)S(1)} %fusion.50) | copy-start | bytes 100
  43.3 7.0 %all-to-all-start.2 = ((bf16[2,2,65536]{2,1,0:T(2,128)(2,1)}), bf16[2,2,65536]{2,1,0:T(2,128)(2,1)}, u32[]{:S(2)}, u32[]{:S(2)}) async-start(bf16[2,2,65536]{2,1,0:T(2,128)(2,1)} %reshape.422), calls=%async_computation.2 | async-start | bytes 1048576 | tf_op jit(solution)/shard_map/all_to_all | solution.py:115
  50.4 7.1 %all-to-all-start = ((f32[1,256,16]{1,0,2:T(1,128)}), f32[1,256,16]{1,0,2:T(1,128)S(1)}, u32[]{:S(2)}, u32[]{:S(2)}) async-start(f32[1,256,16]{1,0,2:T(1,128)} %copy.56), calls=%async_computation | async-start | bytes 32768 | tf_op jit(solution)/shard_map/all_to_all | solution.py:117
  53.6 203.8 %reduce-scatter.3.cloned.1.call-start = ((), (), s32[]{:S(2)}) async-start(), calls=%async_computation.7 | async-start | bytes 786432 | tf_op jit(solution)/shard_map/reduce_scatter | solution.py:151
  75.0 2.0 copy-start.2
  75.0 2.0 copy-start.18
  75.0 2.0 copy-start.34
  75.8 1.4 copy-start
  82.4 1.1 copy-start.10
  82.4 9.5 %copy-start.7 = (f32[256]{0:T(256)}, f32[256]{0:T(256)S(1)}, u32[]{:S(2)}) copy-start(f32[256]{0:T(256)S(1)} %get-tuple-element.920) | copy-start | bytes 3076 | tf_op jit(solution)/shard_map/transpose(jvp())/while
  83.5 8.5 %copy-start.11 = (f32[8]{0:T(128)}, f32[8]{0:T(128)S(1)}, u32[]{:S(2)}) copy-start(f32[8]{0:T(128)S(1)} %get-tuple-element.913) | copy-start | bytes 100 | tf_op jit(solution)/shard_map/transpose(jvp())/while
  86.1 4.1 %copy-start.1 = (f32[256,256]{1,0:T(8,128)}, f32[256,256]{1,0:T(8,128)S(1)}, u32[]{:S(2)}) copy-start(f32[256,256]{1,0:T(8,128)S(1)} %fusion.108) | copy-start | bytes 786436 | tf_op jit(solution)/shard_map/transpose(jvp())/while
  98.3 1.0 copy-start.24
  99.4 1.4 copy-start.5
  99.4 4.7 %copy-start.12 = (f32[2,256,8]{1,2,0:T(8,128)S(1)}, f32[2,256,8]{1,2,0:T(8,128)}, u32[]{:S(2)}) copy-start(f32[2,256,8]{1,2,0:T(8,128)} %get-tuple-element.997) | copy-start | bytes 49156 | tf_op jit(solution)/shard_map/transpose(jvp())/while
  99.4 5.3 %copy-start.19 = (s32[2,256]{1,0:T(2,128)S(1)}, s32[2,256]{1,0:T(2,128)}, u32[]{:S(2)}) copy-start(s32[2,256]{1,0:T(2,128)} %copy-done.18) | copy-start | bytes 6148 | tf_op jit(solution)/shard_map/transpose(jvp())/while
  99.4 5.3 %copy-start.35 = (s32[2]{0:T(128)S(1)}, s32[2]{0:T(128)}, u32[]{:S(2)}) copy-start(s32[2]{0:T(128)} %copy-done.34) | copy-start | bytes 28 | tf_op jit(solution)/shard_map/transpose(jvp())/while
  100.8 3.9 %copy-start.3 = (f32[2,256,256]{2,1,0:T(8,128)S(1)}, f32[2,256,256]{2,1,0:T(8,128)}, u32[]{:S(2)}) copy-start(f32[2,256,256]{2,1,0:T(8,128)} %copy-done.2) | copy-start | bytes 1572868 | tf_op jit(solution)/shard_map/transpose(jvp())/while
  101.4 2.7 %copy-start.6 = (f32[2,256,256]{2,1,0:T(8,128)}, f32[2,256,256]{2,1,0:T(8,128)S(1)}, u32[]{:S(2)}) copy-start(f32[2,256,256]{2,1,0:T(8,128)S(1)} %fusion.113) | copy-start | bytes 1572868 | tf_op jit(solution)/shard_map/transpose(jvp())/while
  104.8 3.0 %copy-start.2 = (f32[2,256,256]{2,1,0:T(8,128)}, f32[2,256,256]{2,1,0:T(8,128)S(1)}, u32[]{:S(2)}) copy-start(f32[2,256,256]{2,1,0:T(8,128)S(1)} %get-tuple-element.1023) | copy-start | bytes 1572868 | tf_op jit(solution)/shard_map/transpose(jvp())/while
  104.8 3.0 %copy-start.18 = (s32[2,256]{1,0:T(2,128)}, s32[2,256]{1,0:T(2,128)S(1)}, u32[]{:S(2)}) copy-start(s32[2,256]{1,0:T(2,128)S(1)} %get-tuple-element.1026) | copy-start | bytes 6148 | tf_op jit(solution)/shard_map/transpose(jvp())/while
  104.8 3.0 %copy-start.34 = (s32[2]{0:T(128)}, s32[2]{0:T(128)S(1)}, u32[]{:S(2)}) copy-start(s32[2]{0:T(128)S(1)} %get-tuple-element.1020) | copy-start | bytes 28 | tf_op jit(solution)/shard_map/transpose(jvp())/while
  106.6 1.4 copy-start
  113.2 1.1 copy-start.10
  113.2 9.5 %copy-start.7 = (f32[256]{0:T(256)}, f32[256]{0:T(256)S(1)}, u32[]{:S(2)}) copy-start(f32[256]{0:T(256)S(1)} %get-tuple-element.920) | copy-start | bytes 3076 | tf_op jit(solution)/shard_map/transpose(jvp())/while
  114.3 8.4 %copy-start.11 = (f32[8]{0:T(128)}, f32[8]{0:T(128)S(1)}, u32[]{:S(2)}) copy-start(f32[8]{0:T(128)S(1)} %get-tuple-element.913) | copy-start | bytes 100 | tf_op jit(solution)/shard_map/transpose(jvp())/while
  116.9 4.1 %copy-start.1 = (f32[256,256]{1,0:T(8,128)}, f32[256,256]{1,0:T(8,128)S(1)}, u32[]{:S(2)}) copy-start(f32[256,256]{1,0:T(8,128)S(1)} %fusion.108) | copy-start | bytes 786436 | tf_op jit(solution)/shard_map/transpose(jvp())/while
  130.1 1.4 copy-start.5
  130.1 4.7 %copy-start.12 = (f32[2,256,8]{1,2,0:T(8,128)S(1)}, f32[2,256,8]{1,2,0:T(8,128)}, u32[]{:S(2)}) copy-start(f32[2,256,8]{1,2,0:T(8,128)} %get-tuple-element.997) | copy-start | bytes 49156 | tf_op jit(solution)/shard_map/transpose(jvp())/while
  130.1 5.3 %copy-start.19 = (s32[2,256]{1,0:T(2,128)S(1)}, s32[2,256]{1,0:T(2,128)}, u32[]{:S(2)}) copy-start(s32[2,256]{1,0:T(2,128)} %copy-done.18) | copy-start | bytes 6148 | tf_op jit(solution)/shard_map/transpose(jvp())/while
  130.2 5.3 %copy-start.35 = (s32[2]{0:T(128)S(1)}, s32[2]{0:T(128)}, u32[]{:S(2)}) copy-start(s32[2]{0:T(128)} %copy-done.34) | copy-start | bytes 28 | tf_op jit(solution)/shard_map/transpose(jvp())/while
  131.5 3.9 %copy-start.3 = (f32[2,256,256]{2,1,0:T(8,128)S(1)}, f32[2,256,256]{2,1,0:T(8,128)}, u32[]{:S(2)}) copy-start(f32[2,256,256]{2,1,0:T(8,128)} %copy-done.2) | copy-start | bytes 1572868 | tf_op jit(solution)/shard_map/transpose(jvp())/while
  132.2 2.7 %copy-start.6 = (f32[2,256,256]{2,1,0:T(8,128)}, f32[2,256,256]{2,1,0:T(8,128)S(1)}, u32[]{:S(2)}) copy-start(f32[2,256,256]{2,1,0:T(8,128)S(1)} %fusion.113) | copy-start | bytes 1572868 | tf_op jit(solution)/shard_map/transpose(jvp())/while
  135.6 4.2 %copy-start.23 = (f32[8]{0:T(128)S(1)}, f32[8]{0:T(128)}, u32[]{:S(2)}) copy-start(f32[8]{0:T(128)} %get-tuple-element.453) | copy-start | bytes 100
  135.6 4.4 %copy-start.31 = (f32[16]{0:T(128)S(1)}, f32[16]{0:T(128)}, u32[]{:S(2)}) copy-start(f32[16]{0:T(128)} %param.19) | copy-start | bytes 196
  135.6 107.7 %copy-start.4 = (bf16[2,256,8,64]{1,3,2,0:T(8,128)(2,1)S(1)}, bf16[2,256,8,64]{1,3,2,0:T(8,128)(2,1)}, u32[]{:S(2)}) copy-start(bf16[2,256,8,64]{1,3,2,0:T(8,128)(2,1)} %get-tuple-element.448) | copy-start | bytes 1572868
  135.6 123.4 %reduce-scatter.5.cloned.1.call-start = ((), (), s32[]{:S(2)}) async-start(), calls=%async_computation.8 | async-start | bytes 786432 | tf_op jit(solution)/shard_map/reduce_scatter | solution.py:152
  140.1 109.4 %all-to-all-start.4 = ((f32[2,1,2048]{2,1,0:T(1,128)}), f32[2,1,2048]{2,1,0:T(1,128)S(1)}, u32[]{:S(2)}, u32[]{:S(2)}) async-start(f32[2,1,2048]{2,1,0:T(1,128)} %reshape.426), calls=%async_computation.6 | async-start | bytes 32768 | tf_op jit(solution)/shard_map/all_to_all | solution.py:149
  249.5 6.0 %all-to-all-start.3 = ((bf16[2,2,65536]{2,1,0:T(2,128)(2,1)}), bf16[2,2,65536]{2,1,0:T(2,128)(2,1)S(1)}, u32[]{:S(2)}, u32[]{:S(2)}) async-start(bf16[2,2,65536]{2,1,0:T(2,128)(2,1)} %reshape.424), calls=%async_computation.3 | async-start | bytes 1048576 | tf_op jit(solution)/shard_map/all_to_all | solution.py:142
  (13 other events, 9.6 us)
Sparse Core Ops, SparseCore 0:
  135.7 16.2 reduce-scatter.2
  155.1 17.3 reduce-scatter.4
where the time goes:
time: 269 us; the launch traced here: 267 us
  blocking collectives  106 us (39%)
  other arithmetic  44.1 us (16%)
  local copies, waits for them, and re-layouts  38.4 us (14%)
  matrix products  32.5 us (12%)
  starting transfers between devices  26 us (10%)
  between operations  14.4 us (5%)
  loops' own time  5.8 us (2%)
    psum x1, blocking collectives, on_device(): lax.psum((partial_sums[0], partial_sums[1], partial_sums[2]), ('dp', 'ctx'))  99.9 us
    unnamed x54, local copies, waits for them, and re-layouts  17.9 us
    dot_general x4, matrix products, advance(): result = jnp.einsum('ijh,jhp->ihp', mixing, in_block, precision=highest)  15.2 us
    unnamed x7, other arithmetic  13.7 us
    all_to_all x1, starting transfers between devices, on_device(): lax.all_to_all(head_inputs, 'ctx', split_axis=2, concat_axis=1, tiled=True)  10.5 us
    another operation x17, other arithmetic  9.32 us
    dot_general x6, matrix products, advance(): jnp.einsum('jh,jhp,jn->hpn', tail, in_block, write_block, precision=highest)  7.06 us
    dot_general x6, matrix products, advance(): jnp.einsum('in,hpn->ihp', read_block, state, precision=highest)  6.04 us
  transfers between devices with their start and end apart: 7, of which 0 were waited for; matrix products, arithmetic and copies ran while one was open for 12% of the time, Pallas kernels for 0%

commit v1 on v0

--- a/solution.py
+++ b/solution.py
@@ -161,7 +161,7 @@
 
     partial_sums = (place(grads[4]), place(grads[5]), place(grads[6]))
     total_rate, total_bias, total_skip = lax.psum(
-        (partial_sums[0], partial_sums[1], partial_sums[2]), ("dp", "ctx")
+        lax.psum((partial_sums[0], partial_sums[1], partial_sums[2]), "dp"), "ctx"
     )
     return (out_inputs, out_write, out_read, out_step, total_rate, total_bias, total_skip)
 

time: 269 us -> 863 us (3.21)
  blocking collectives: 106 us -> 700 us
    psum x1 -> x2, blocking collectives: 99.9 us -> 694 us  [the longest x1 581 us: on_device(): lax.psum((partial_sums[0], partial_sums[1], partial_sums[2]), 'dp')]
  transfers between devices with their start and end apart: 7 -> 7, of which waited for: 0 -> 0; matrix products, arithmetic and copies ran while one was open for 12% -> 4% of each run, Pallas kernels for 0% -> 0%
where the time goes in v1:
time: 863 us; the launch traced here: 861 us
  blocking collectives  700 us (81%)
  other arithmetic  44.1 us (5%)
  local copies, waits for them, and re-layouts  38.4 us (4%)
  matrix products  32.5 us (4%)
  starting transfers between devices  25.4 us (3%)
  between operations  14.4 us (2%)
    psum x1, blocking collectives, on_device(): lax.psum((partial_sums[0], partial_sums[1], partial_sums[2]), 'dp')  581 us
    psum x1, blocking collectives, on_device(): lax.psum(lax.psum((partial_sums[0], partial_sums[1], partial_sums[2]), 'd...  113 us
    unnamed x54, local copies, waits for them, and re-layouts  17.9 us
  transfers between devices with their start and end apart: 7, of which 0 were waited for; matrix products, arithmetic and copies ran while one was open for 4% of the time, Pallas kernels for 0%

profile of v1, /device:TPU:1, one launch (start us, length us, event | category | flops | bytes accessed | tf_op | source)
XLA Modules:
  0.0 861.5 jit_solution(13816192471839117244)
XLA Ops:
  7.2 2.4 copy.57
  10.2 3.9 reduce.18
  15.0 10.5 %all-to-all-start.1 = ((bf16[2,2,65536]{2,1,0:T(2,128)(2,1)}), bf16[2,2,65536]{2,1,0:T(2,128)(2,1)S(1)}, u32[]{:S(2)}, u32[]{:S(2)}) async-start(bf16[2,2,65536]{2,1,0:T(2,128)(2,1)} %reshape.420), calls=%async_computation.1 | async-start | bytes 1048576 | tf_op jit(solution)/shard_map/all_to_all | solution.py:114
  26.2 1.8 all_gather.9
  30.4 2.0 all_gather.10
  32.4 2.0 all_gather.11
  34.4 2.4 copy.58
  36.8 4.7 reduce.19
  41.5 1.8 reshape.422
  43.3 4.4 all-to-all-start.2
  48.2 1.1 convert_bitcast_fusion.1
  49.3 1.1 copy.72
  50.4 3.3 all-to-all-start
  53.8 1.4 reshape.423
  55.3 1.1 convert_bitcast_fusion
  56.4 1.1 copy.73
  58.1 13.2 %while.44 = (s32[]{:T(128)}, f32[8,64,256]{2,1,0:T(8,128)S(1)}, s32[]{:T(128)}, f32[2,8,64,256]{3,2,1,0:T(8,128)}, s32[2]{0:T(128)S(1)}, /*index=5*/f32[2,256,8]...) while((s32[]{:T(128)}, f32[8,64,256]{2,1,0:T(8,128)S(1)}, ...), condition=%wide.region_3.4_spmd.clone, body=%wide.region_0.3_spmd.clone.sunk | while | flops 403577376 | bytes 2971505 | solution.py:58
  62.8 1.9 convolution_add_fusion.6
  69.4 1.9 convolution_add_fusion.6
  75.0 60.5 %while.45 = (s32[]{:T(128)}, f32[8]{0:T(128)}, f32[8,64,256]{2,1,0:T(8,128)}, bf16[2,256,8,64]{1,3,2,0:T(8,128)(2,1)}, f32[2,256,256]{2,1,0:T(8,128)}, /*index=5...) while((s32[]{:T(128)}, f32[8]{0:T(128)}, ...), condition=%wide.region_17.18_spmd.clone, body=%wide.region_4.0_spmd.clone.sunk | while | flops 3434652672 | bytes 35708892 | solution.py:58
  75.8 1.2 dynamic-slice_bitcast_fusion.14
  77.2 1.1 dynamic-slice_bitcast_fusion.15
  81.1 1.3 compare_convert_fusion.6
  86.1 4.1 fusion.109
  90.2 1.1 fusion.114
  93.4 1.4 bitcast_dynamic-update-slice_fusion.7
  94.8 3.6 fusion.112
  99.4 1.4 convolution_add_fusion.7
  101.4 2.5 reduce-window.70
  105.5 1.1 broadcast_select_fusion.3
  106.6 1.2 dynamic-slice_bitcast_fusion.14
  108.0 1.1 dynamic-slice_bitcast_fusion.15
  111.9 1.3 compare_convert_fusion.6
  116.9 4.0 fusion.109
  120.9 1.1 fusion.114
  124.1 1.4 bitcast_dynamic-update-slice_fusion.7
  125.5 3.6 fusion.112
  130.2 1.4 convolution_add_fusion.7
  132.2 2.5 reduce-window.70
  137.2 1.3 reduce.21
  139.2 3.5 all-to-all-start.4
  144.0 3.9 reduce.20
  147.8 1.1 reshape.424
  148.9 3.5 all-to-all-start.3
  157.0 581.2 %all-reduce.2 = (f32[16]{0:T(128)S(1)}, f32[16]{0:T(128)S(1)}, f32[16]{0:T(128)S(1)}) all-reduce(f32[16]{0:T(128)S(1)} %multiply_dynamic-update-slice_fusion, f32[16]{0:T(128)S(1)} %dynamic_update_slice.66, f32[16]{0:T(128)S(1)} %dynamic_update_slice.67), channel_id=1, replica_groups=mesh['dp'=256,'ctx'=2] {'dp'}, use_global_device_ids=true, to_apply=%region_21.22 | all-reduce | flops 48 | bytes 384 | tf_op jit(solution)/shard_map/psum | solution.py:164
  738.2 113.2 %all-reduce.3 = (f32[16]{0:T(128)}, f32[16]{0:T(128)}, f32[16]{0:T(128)}) all-reduce(f32[16]{0:T(128)S(1)} %get-tuple-element.671, f32[16]{0:T(128)S(1)} %get-tuple-element.672, f32[16]{0:T(128)S(1)} %get-tuple-element.673), channel_id=1, replica_groups=mesh['dp'=256,'ctx'=2] {'ctx'}, use_global_device_ids=true, to_apply=%region_22.23 | all-reduce | flops 48 | bytes 384 | tf_op jit(solution)/shard_map/psum | solution.py:163
  851.4 1.6 convert_element_type.114
  853.0 1.6 convert_element_type.115
  (253 shorter events, 45.6 us)
Async XLA Ops:
  14.0 11.4 %copy-start.32 = (f32[16]{0:T(128)S(1)}, f32[16]{0:T(128)}, u32[]{:S(2)}) copy-start(f32[16]{0:T(128)} %param.20) | copy-start | bytes 196
  14.1 11.5 %copy-start.30 = (f32[16]{0:T(128)S(1)}, f32[16]{0:T(128)}, u32[]{:S(2)}) copy-start(f32[16]{0:T(128)} %param.19) | copy-start | bytes 196
  14.1 11.6 %copy-start.33 = (f32[16]{0:T(128)S(1)}, f32[16]{0:T(128)}, u32[]{:S(2)}) copy-start(f32[16]{0:T(128)} %param.21) | copy-start | bytes 196
  14.1 12.2 %copy-start.29 = (s32[1,256]{1,0:T(1,128)S(1)}, s32[1,256]{1,0:T(1,128)}, u32[]{:S(2)}) copy-start(s32[1,256]{1,0:T(1,128)} %param.18) | copy-start | bytes 3076
  14.1 15.6 %copy-start.20 = (f32[1,256,16]{1,2,0:T(8,128)S(1)}, f32[1,256,16]{1,2,0:T(8,128)}, u32[]{:S(2)}) copy-start(f32[1,256,16]{1,2,0:T(8,128)} %param.17) | copy-start | bytes 49156
  14.1 16.3 %copy-start.16 = (bf16[1,256,256]{2,1,0:T(8,128)(2,1)S(1)}, bf16[1,256,256]{2,1,0:T(8,128)(2,1)}, u32[]{:S(2)}) copy-start(bf16[1,256,256]{2,1,0:T(8,128)(2,1)} %param.15) | copy-start | bytes 393220
  15.0 17.4 %copy-start.17 = (bf16[1,256,256]{2,1,0:T(8,128)(2,1)S(1)}, bf16[1,256,256]{2,1,0:T(8,128)(2,1)}, u32[]{:S(2)}) copy-start(bf16[1,256,256]{2,1,0:T(8,128)(2,1)} %param.16) | copy-start | bytes 393220
  15.0 28.3 %all-to-all-start.1 = ((bf16[2,2,65536]{2,1,0:T(2,128)(2,1)}), bf16[2,2,65536]{2,1,0:T(2,128)(2,1)S(1)}, u32[]{:S(2)}, u32[]{:S(2)}) async-start(bf16[2,2,65536]{2,1,0:T(2,128)(2,1)} %reshape.420), calls=%async_computation.1 | async-start | bytes 1048576 | tf_op jit(solution)/shard_map/all_to_all | solution.py:114
  25.6 31.9 %copy-start.25 = (f32[8]{0:T(128)}, f32[8]{0:T(128)S(1)}, u32[]{:S(2)}) copy-start(f32[8]{0:T(128)S(1)} %dynamic_slice.111) | copy-start | bytes 100
  25.6 31.8 %copy-start.27 = (f32[8]{0:T(128)}, f32[8]{0:T(128)S(1)}, u32[]{:S(2)}) copy-start(f32[8]{0:T(128)S(1)} %fusion.50) | copy-start | bytes 100
  43.3 7.0 all-to-all-start.2
  50.4 7.1 all-to-all-start
  53.6 797.8 %reduce-scatter.3.cloned.1.call-start = ((), (), s32[]{:S(2)}) async-start(), calls=%async_computation.7 | async-start | bytes 786432 | tf_op jit(solution)/shard_map/reduce_scatter | solution.py:151
  75.0 2.0 copy-start.2
  75.0 2.0 copy-start.18
  75.0 2.0 copy-start.34
  75.8 1.4 copy-start
  82.4 1.1 copy-start.10
  82.4 9.5 %copy-start.7 = (f32[256]{0:T(256)}, f32[256]{0:T(256)S(1)}, u32[]{:S(2)}) copy-start(f32[256]{0:T(256)S(1)} %get-tuple-element.923) | copy-start | bytes 3076 | tf_op jit(solution)/shard_map/transpose(jvp())/while
  83.5 8.5 copy-start.11
  86.1 4.1 copy-start.1
  98.3 1.0 copy-start.24
  99.4 1.4 copy-start.5
  99.4 4.7 copy-start.12
  99.4 5.3 copy-start.19
  99.4 5.3 copy-start.35
  100.8 3.9 copy-start.3
  101.4 2.7 copy-start.6
  104.8 3.0 copy-start.2
  104.8 3.0 copy-start.18
  104.8 3.0 copy-start.34
  106.6 1.4 copy-start
  113.2 1.1 copy-start.10
  113.2 9.5 %copy-start.7 = (f32[256]{0:T(256)}, f32[256]{0:T(256)S(1)}, u32[]{:S(2)}) copy-start(f32[256]{0:T(256)S(1)} %get-tuple-element.923) | copy-start | bytes 3076 | tf_op jit(solution)/shard_map/transpose(jvp())/while
  114.3 8.4 copy-start.11
  116.9 4.1 copy-start.1
  130.1 1.4 copy-start.5
  130.1 4.7 copy-start.12
  130.1 5.3 copy-start.19
  130.2 5.3 copy-start.35
  131.5 3.9 copy-start.3
  132.2 2.7 copy-start.6
  135.6 7.2 copy-start.4
  135.6 717.4 %reduce-scatter.5.cloned.1.call-start = ((), (), s32[]{:S(2)}) async-start(), calls=%async_computation.8 | async-start | bytes 786432 | tf_op jit(solution)/shard_map/reduce_scatter | solution.py:152
  139.2 9.7 %all-to-all-start.4 = ((f32[2,1,2048]{2,1,0:T(1,128)}), f32[2,1,2048]{2,1,0:T(1,128)S(1)}, u32[]{:S(2)}, u32[]{:S(2)}) async-start(f32[2,1,2048]{2,1,0:T(1,128)} %reshape.426), calls=%async_computation.6 | async-start | bytes 32768 | tf_op jit(solution)/shard_map/all_to_all | solution.py:149
  148.9 5.4 all-to-all-start.3
  154.9 1.7 copy-start.23
  154.9 1.9 copy-start.31
  (13 other events, 9.4 us)
Sparse Core Ops, SparseCore 0:
  135.7 16.2 reduce-scatter.2
  155.0 17.3 reduce-scatter.4
